TPU v7x, 32 devices: a whole 2x2x4 slice. The times are simulated.
32 devices in a mesh: sec: 8 (over y, x, core), cross: 4 (over z).
Axes of the slice: x: 2, y: 2, z: 4, core: 2. Of those that a mesh axis runs over, the one named last changes fastest.
Arguments:
- rhs_field: float32 [2, 8, 2, 512, 512], P(None, 'sec', None, 'cross'), may hold values from -1.5 to 1.5
- slowness: float32 [8, 512, 512], P('sec', 'cross'), may hold values from 0.25 to 4
- absorb_depth: int32 [8], P('sec'), may hold values from 8 to 64
- line_inverse: bfloat16 [8, 2, 512, 512], P('sec'), may hold values from -1 to 1
- cross_inverse: bfloat16 [8, 2, 512, 512], P('sec', None, 'cross'), may hold values from -1 to 1
Outputs:
- solution: float32 [2, 8, 2, 512, 512], P(None, 'sec', None, 'cross')
- residual: float32 [2, 8, 2, 512, 512], P(None, 'sec', None, 'cross')
All inputs are finite; a program needn't handle non-finite values.
Results may differ from a plain program's by a relative error of at most 0.02.
Values may be sent and summed in bfloat16 or wider, within the bound.
A program may use at most 64 MiB of HBM per device.

v0:
```python
import jax
import jax.numpy as jnp
from jax import lax
from jax.sharding import PartitionSpec as P

SIGMA_TOP = 2.0
CENTER = 128.0 / 30.0
FACE = 14.0 / 30.0
EDGE = 3.0 / 30.0
CORNER = 1.0 / 30.0


def passed_along(shard, axis, by):
    devices = lax.axis_size(axis)
    pairs = [(i, i + by) for i in range(devices) if 0 <= i + by < devices]
    return lax.ppermute(shard, axis, pairs)


def with_halo(cells, sides, width):
    for axis, dim in sides:
        count = lax.axis_size(axis)
        ends = count - 1
        head = lax.slice_in_dim(cells, 0, width, axis=dim)
        tail = lax.slice_in_dim(cells, cells.shape[dim] - width, cells.shape[dim], axis=dim)
        cells = jnp.concatenate(
            [
                lax.ppermute(tail, axis, [(i, (i + 1) % count) for i in range(ends)]),
                cells,
                lax.ppermute(head, axis, [((i + 1) % count, i) for i in range(ends)]),
            ],
            axis=dim,
        )
    return cells


def complex_line(source, matrix):
    real_part = jnp.dot(source[0], matrix[0], preferred_element_type=jnp.float32) - jnp.dot(
        source[1], matrix[1], preferred_element_type=jnp.float32
    )
    imag_part = jnp.dot(source[0], matrix[1], preferred_element_type=jnp.float32) + jnp.dot(
        source[1], matrix[0], preferred_element_type=jnp.float32
    )
    return jnp.stack([real_part, imag_part]).astype(jnp.bfloat16)


def cross_fold(mixed, coupling_rows):
    gathered = lax.all_gather(mixed, "cross", axis=2, tiled=True)
    real_real = jnp.einsum(
        "yk,rkx->ryx", coupling_rows[0], gathered[0], preferred_element_type=jnp.float32
    )
    imag_imag = jnp.einsum(
        "yk,rkx->ryx", coupling_rows[1], gathered[1], preferred_element_type=jnp.float32
    )
    real_imag = jnp.einsum(
        "yk,rkx->ryx", coupling_rows[0], gathered[1], preferred_element_type=jnp.float32
    )
    imag_real = jnp.einsum(
        "yk,rkx->ryx", coupling_rows[1], gathered[0], preferred_element_type=jnp.float32
    )
    real_part = real_real - imag_imag
    imag_part = real_imag + imag_real
    return jnp.stack([real_part, imag_part])


def sweep_section(rhs_local, prior, line_matrix, cross_local):
    item_count = rhs_local.shape[2]
    line_count = rhs_local.shape[3]
    column_count = rhs_local.shape[4]
    source = (rhs_local[:, 0] + prior).astype(jnp.bfloat16)
    mixed = complex_line(source.reshape(2, item_count * line_count, column_count), line_matrix)
    mixed = mixed.reshape(2, item_count, line_count, column_count)
    prior = cross_fold(mixed, cross_local[0])
    outputs = [prior]
    return jnp.stack(outputs, axis=1)


def absorption(absorb_depth, column_count):
    column = jnp.arange(column_count, dtype=jnp.int32)
    distance = jnp.minimum(column, column_count - 1 - column).astype(jnp.float32)
    depth = absorb_depth.astype(jnp.float32)[:, None]
    ramp = jnp.maximum(depth - distance[None, :], 0.0) / depth
    return SIGMA_TOP * ramp * ramp


def operate(field, padded, slowness, absorb_depth):
    layer_count = field.shape[1]
    line_count = field.shape[3]
    column_count = field.shape[4]
    weights = (0.0, FACE, EDGE, CORNER)
    near = jnp.zeros(field.shape, jnp.float32)
    for depth_move in (-1, 0, 1):
        for line_move in (-1, 0, 1):
            for column_move in (-1, 0, 1):
                reach = abs(depth_move) + abs(line_move) + abs(column_move)
                if reach > 0:
                    near = (
                        near
                        + weights[reach]
                        * padded[
                            :,
                            1 + depth_move : 1 + depth_move + layer_count,
                            :,
                            1 + line_move : 1 + line_move + line_count,
                            1 + column_move : 1 + column_move + column_count,
                        ]
                    )
    damping = absorption(absorb_depth, column_count)
    wave_real = slowness[:, None, :, :]
    wave_imag = wave_real * damping[:, None, None, :]
    real_part = CENTER * field[0] - near[0] - (wave_real * field[0] - wave_imag * field[1])
    imag_part = CENTER * field[1] - near[1] - (wave_real * field[1] + wave_imag * field[0])
    return jnp.stack([real_part, imag_part])


def per_device(rhs_field, slowness, absorb_depth, line_inverse, cross_inverse):
    line_matrix = line_inverse[0]
    layer_count = rhs_field.shape[1]
    item_count = rhs_field.shape[2]
    line_count = rhs_field.shape[3]
    column_count = rhs_field.shape[4]
    sections = lax.axis_size("sec")
    start_prior = jnp.zeros((2, item_count, line_count, column_count), jnp.float32)
    first = sweep_section(rhs_field, start_prior, line_matrix, cross_inverse)

    def advance_whole(counter, current):
        prior = passed_along(current[:, layer_count - 1].astype(jnp.bfloat16), "sec", 1).astype(
            jnp.float32
        )
        return sweep_section(rhs_field, prior, line_matrix, cross_inverse)

    solution = lax.fori_loop(0, sections - 1, advance_whole, first)
    padded = with_halo(solution.astype(jnp.bfloat16), (("sec", 1), ("cross", 3)), 1).astype(
        solution.dtype
    )
    padded = jnp.pad(padded, ((0, 0), (0, 0), (0, 0), (0, 0), (1, 1)))
    residual = rhs_field - operate(solution, padded, slowness, absorb_depth)
    return (solution, residual)


def solution(mesh):
    placed = (
        P(None, "sec", None, "cross", None),
        P("sec", "cross", None),
        P("sec"),
        P("sec", None, None, None),
        P("sec", None, "cross", None),
    )
    return jax.shard_map(
        per_device,
        mesh=mesh,
        in_specs=placed,
        out_specs=(P(None, "sec", None, "cross", None), P(None, "sec", None, "cross", None)),
        check_vma=False,
    )
```

profile of v0, /device:TPU:29, one launch (start us, length us, event | category | flops | bytes accessed | tf_op | source)
XLA Modules:
  0.0 550.5 jit_solution(8735741020299506886)
XLA Ops:
  7.2 1.4 convert_element_type.39
  9.8 1.0 fusion.28
  10.8 1.2 copy.21
  13.2 44.2 %all-gather.3.cloned.1.call-done = bf16[2,2,512,512]{2,3,1,0:T(8,128)(2,1)} async-done(((bf16[2,2,128,512]{2,3,1,0:T(8,128)(2,1)}), bf16[2,2,512,512]{2,3,1,0:T(8,128)(2,1)}) %all-gather.3.cloned.1.call-update) | async-done | bytes 2097168 | tf_op jit(solution)/shard_map/all_gather | solution.py:47
  57.4 1.8 fusion.72
  59.2 1.7 fusion.73
  61.8 452.2 %while.10 = (s32[]{:T(128)}, f32[2,1,2,128,512]{3,4,2,0,1:T(8,128)S(1)}, f32[2,1,2,128,512]{3,4,2,0,1:T(8,128)S(1)}, bf16[2,512,512]{2,1,0:T(8,128)(2,1)S(1)}, bf16[1,2,128,512]{3,2,1,0:T(8,128)(2,1)}, /*index=5*/s32[]{:T(128)}) while((s32[]{:T(128)}, f32[2,1,2,128,512]{3,4,2,0,1:T(8,128)S(1)}, f32[2,1,2,128,512]{3,4,2,0,1:T(8,128)S(1)}, ...), condition=%wide.region_1.0_spmd, body=%wide.region_0.0_spmd.sunk | while | flops 1075838976 | bytes 44040396 | solution.py:131
  61.9 1.0 copy.32
  62.9 3.6 collective-permute-start
  66.8 6.1 %collective-permute-done = bf16[2,2,128,512]{3,2,1,0:T(8,128)(2,1)} collective-permute-done((bf16[2,2,128,512]{3,2,1,0:T(8,128)(2,1)}, bf16[2,2,128,512]{3,2,1,0:T(8,128)(2,1)}, u32[]{:S(2)}, u32[]{:S(2)}) %collective-permute-start) | collective-permute-done | bytes 524320 | tf_op jit(solution)/shard_map/while/body/eval_jaxpr/ppermute | solution.py:16
  72.9 1.2 fusion.142
  76.6 45.4 %all-gather.5.cloned.1.call-done = bf16[2,2,512,512]{2,3,1,0:T(8,128)(2,1)} async-done(((bf16[2,2,128,512]{2,3,1,0:T(8,128)(2,1)}), bf16[2,2,512,512]{2,3,1,0:T(8,128)(2,1)}) %all-gather.5.cloned.1.call-update) | async-done | bytes 2097168 | tf_op jit(solution)/shard_map/while/body/eval_jaxpr/all_gather | solution.py:47
  122.0 1.8 fusion.150
  123.8 1.7 fusion.148
  126.5 1.0 copy.32
  127.5 3.6 collective-permute-start
  131.4 6.1 %collective-permute-done = bf16[2,2,128,512]{3,2,1,0:T(8,128)(2,1)} collective-permute-done((bf16[2,2,128,512]{3,2,1,0:T(8,128)(2,1)}, bf16[2,2,128,512]{3,2,1,0:T(8,128)(2,1)}, u32[]{:S(2)}, u32[]{:S(2)}) %collective-permute-start) | collective-permute-done | bytes 524320 | tf_op jit(solution)/shard_map/while/body/eval_jaxpr/ppermute | solution.py:16
  137.5 1.2 fusion.142
  141.2 45.4 %all-gather.5.cloned.1.call-done = bf16[2,2,512,512]{2,3,1,0:T(8,128)(2,1)} async-done(((bf16[2,2,128,512]{2,3,1,0:T(8,128)(2,1)}), bf16[2,2,512,512]{2,3,1,0:T(8,128)(2,1)}) %all-gather.5.cloned.1.call-update) | async-done | bytes 2097168 | tf_op jit(solution)/shard_map/while/body/eval_jaxpr/all_gather | solution.py:47
  186.6 1.8 fusion.150
  188.4 1.7 fusion.148
  191.1 1.0 copy.32
  192.1 3.6 collective-permute-start
  196.0 6.1 %collective-permute-done = bf16[2,2,128,512]{3,2,1,0:T(8,128)(2,1)} collective-permute-done((bf16[2,2,128,512]{3,2,1,0:T(8,128)(2,1)}, bf16[2,2,128,512]{3,2,1,0:T(8,128)(2,1)}, u32[]{:S(2)}, u32[]{:S(2)}) %collective-permute-start) | collective-permute-done | bytes 524320 | tf_op jit(solution)/shard_map/while/body/eval_jaxpr/ppermute | solution.py:16
  202.1 1.2 fusion.142
  205.8 45.4 %all-gather.5.cloned.1.call-done = bf16[2,2,512,512]{2,3,1,0:T(8,128)(2,1)} async-done(((bf16[2,2,128,512]{2,3,1,0:T(8,128)(2,1)}), bf16[2,2,512,512]{2,3,1,0:T(8,128)(2,1)}) %all-gather.5.cloned.1.call-update) | async-done | bytes 2097168 | tf_op jit(solution)/shard_map/while/body/eval_jaxpr/all_gather | solution.py:47
  251.2 1.8 fusion.150
  253.0 1.7 fusion.148
  255.7 1.0 copy.32
  256.7 3.6 collective-permute-start
  260.6 6.1 %collective-permute-done = bf16[2,2,128,512]{3,2,1,0:T(8,128)(2,1)} collective-permute-done((bf16[2,2,128,512]{3,2,1,0:T(8,128)(2,1)}, bf16[2,2,128,512]{3,2,1,0:T(8,128)(2,1)}, u32[]{:S(2)}, u32[]{:S(2)}) %collective-permute-start) | collective-permute-done | bytes 524320 | tf_op jit(solution)/shard_map/while/body/eval_jaxpr/ppermute | solution.py:16
  266.7 1.2 fusion.142
  270.4 45.4 %all-gather.5.cloned.1.call-done = bf16[2,2,512,512]{2,3,1,0:T(8,128)(2,1)} async-done(((bf16[2,2,128,512]{2,3,1,0:T(8,128)(2,1)}), bf16[2,2,512,512]{2,3,1,0:T(8,128)(2,1)}) %all-gather.5.cloned.1.call-update) | async-done | bytes 2097168 | tf_op jit(solution)/shard_map/while/body/eval_jaxpr/all_gather | solution.py:47
  315.8 1.8 fusion.150
  317.6 1.7 fusion.148
  320.3 1.0 copy.32
  321.3 3.6 collective-permute-start
  325.2 6.1 %collective-permute-done = bf16[2,2,128,512]{3,2,1,0:T(8,128)(2,1)} collective-permute-done((bf16[2,2,128,512]{3,2,1,0:T(8,128)(2,1)}, bf16[2,2,128,512]{3,2,1,0:T(8,128)(2,1)}, u32[]{:S(2)}, u32[]{:S(2)}) %collective-permute-start) | collective-permute-done | bytes 524320 | tf_op jit(solution)/shard_map/while/body/eval_jaxpr/ppermute | solution.py:16
  331.3 1.2 fusion.142
  335.0 45.4 %all-gather.5.cloned.1.call-done = bf16[2,2,512,512]{2,3,1,0:T(8,128)(2,1)} async-done(((bf16[2,2,128,512]{2,3,1,0:T(8,128)(2,1)}), bf16[2,2,512,512]{2,3,1,0:T(8,128)(2,1)}) %all-gather.5.cloned.1.call-update) | async-done | bytes 2097168 | tf_op jit(solution)/shard_map/while/body/eval_jaxpr/all_gather | solution.py:47
  380.4 1.8 fusion.150
  382.2 1.7 fusion.148
  384.9 1.0 copy.32
  385.9 3.6 collective-permute-start
  389.8 6.1 %collective-permute-done = bf16[2,2,128,512]{3,2,1,0:T(8,128)(2,1)} collective-permute-done((bf16[2,2,128,512]{3,2,1,0:T(8,128)(2,1)}, bf16[2,2,128,512]{3,2,1,0:T(8,128)(2,1)}, u32[]{:S(2)}, u32[]{:S(2)}) %collective-permute-start) | collective-permute-done | bytes 524320 | tf_op jit(solution)/shard_map/while/body/eval_jaxpr/ppermute | solution.py:16
  395.9 1.2 fusion.142
  399.6 45.4 %all-gather.5.cloned.1.call-done = bf16[2,2,512,512]{2,3,1,0:T(8,128)(2,1)} async-done(((bf16[2,2,128,512]{2,3,1,0:T(8,128)(2,1)}), bf16[2,2,512,512]{2,3,1,0:T(8,128)(2,1)}) %all-gather.5.cloned.1.call-update) | async-done | bytes 2097168 | tf_op jit(solution)/shard_map/while/body/eval_jaxpr/all_gather | solution.py:47
  445.0 1.8 fusion.150
  446.8 1.7 fusion.148
  449.5 1.0 copy.32
  450.5 3.6 collective-permute-start
  454.4 6.1 %collective-permute-done = bf16[2,2,128,512]{3,2,1,0:T(8,128)(2,1)} collective-permute-done((bf16[2,2,128,512]{3,2,1,0:T(8,128)(2,1)}, bf16[2,2,128,512]{3,2,1,0:T(8,128)(2,1)}, u32[]{:S(2)}, u32[]{:S(2)}) %collective-permute-start) | collective-permute-done | bytes 524320 | tf_op jit(solution)/shard_map/while/body/eval_jaxpr/ppermute | solution.py:16
  460.5 1.2 fusion.142
  464.2 45.4 %all-gather.5.cloned.1.call-done = bf16[2,2,512,512]{2,3,1,0:T(8,128)(2,1)} async-done(((bf16[2,2,128,512]{2,3,1,0:T(8,128)(2,1)}), bf16[2,2,512,512]{2,3,1,0:T(8,128)(2,1)}) %all-gather.5.cloned.1.call-update) | async-done | bytes 2097168 | tf_op jit(solution)/shard_map/while/body/eval_jaxpr/all_gather | solution.py:47
  509.6 1.8 fusion.150
  511.4 1.7 fusion.148
  514.5 3.7 collective-permute-start.1
  518.2 1.9 collective-permute-start.2
  520.8 5.5 collective-permute-done.1
  526.3 2.7 collective-permute-done.2
  529.1 1.3 collective-permute-start.3
  530.4 4.0 collective-permute-start.4
  535.8 5.4 fusion.68
  542.5 1.2 maximum_subtract_fusion
  (161 shorter events, 32.7 us)
Async XLA Ops:
  7.2 1.5 copy-start
  7.2 50.2 %all-gather.3.cloned.1.call-start = ((), (), s32[]{:S(2)}) async-start(), calls=%async_computation | async-start | bytes 2621440 | tf_op jit(solution)/shard_map/all_gather | solution.py:47
  9.6 3.2 copy-start.4
  10.8 46.6 %copy-start.2 = (bf16[1,2,128,512]{3,2,1,0:T(8,128)(2,1)S(1)}, bf16[1,2,128,512]{3,2,1,0:T(8,128)(2,1)}, u32[]{:S(2)}) copy-start(bf16[1,2,128,512]{3,2,1,0:T(8,128)(2,1)} %param.11) | copy-start | bytes 786436
  57.4 3.5 copy-start.7
  61.8 60.2 %all-gather.5.cloned.1.call-start = ((), (), s32[]{:S(2)}) async-start(), calls=%async_computation.1 | async-start | bytes 2621440 | tf_op jit(solution)/shard_map/while/body/eval_jaxpr/all_gather | solution.py:47
  62.9 10.0 %collective-permute-start = (bf16[2,2,128,512]{3,2,1,0:T(8,128)(2,1)}, bf16[2,2,128,512]{3,2,1,0:T(8,128)(2,1)}, u32[]{:S(2)}, u32[]{:S(2)}) collective-permute-start(bf16[2,2,128,512]{3,2,1,0:T(8,128)(2,1)} %bitcast.168), channel_id=1, source_target_pairs={{0,4},{4,8},{8,12},{12,16},{16,20},{20,24},{24,28},{1,5},{5,9},{9,... | collective-permute-start | bytes 1572872 | tf_op jit(solution)/shard_map/while/body/eval_jaxpr/ppermute | solution.py:16
  75.6 46.4 %copy-start.3 = (bf16[1,2,128,512]{3,2,1,0:T(8,128)(2,1)S(1)}, bf16[1,2,128,512]{3,2,1,0:T(8,128)(2,1)}, u32[]{:S(2)}) copy-start(bf16[1,2,128,512]{3,2,1,0:T(8,128)(2,1)} %get-tuple-element.113) | copy-start | bytes 786436 | tf_op jit(solution)/shard_map/while
  122.0 3.5 copy-start.1
  126.4 60.2 %all-gather.5.cloned.1.call-start = ((), (), s32[]{:S(2)}) async-start(), calls=%async_computation.1 | async-start | bytes 2621440 | tf_op jit(solution)/shard_map/while/body/eval_jaxpr/all_gather | solution.py:47
  127.5 10.0 %collective-permute-start = (bf16[2,2,128,512]{3,2,1,0:T(8,128)(2,1)}, bf16[2,2,128,512]{3,2,1,0:T(8,128)(2,1)}, u32[]{:S(2)}, u32[]{:S(2)}) collective-permute-start(bf16[2,2,128,512]{3,2,1,0:T(8,128)(2,1)} %bitcast.168), channel_id=1, source_target_pairs={{0,4},{4,8},{8,12},{12,16},{16,20},{20,24},{24,28},{1,5},{5,9},{9,... | collective-permute-start | bytes 1572872 | tf_op jit(solution)/shard_map/while/body/eval_jaxpr/ppermute | solution.py:16
  140.2 46.4 %copy-start.3 = (bf16[1,2,128,512]{3,2,1,0:T(8,128)(2,1)S(1)}, bf16[1,2,128,512]{3,2,1,0:T(8,128)(2,1)}, u32[]{:S(2)}) copy-start(bf16[1,2,128,512]{3,2,1,0:T(8,128)(2,1)} %get-tuple-element.113) | copy-start | bytes 786436 | tf_op jit(solution)/shard_map/while
  186.6 3.5 copy-start.1
  191.1 60.2 %all-gather.5.cloned.1.call-start = ((), (), s32[]{:S(2)}) async-start(), calls=%async_computation.1 | async-start | bytes 2621440 | tf_op jit(solution)/shard_map/while/body/eval_jaxpr/all_gather | solution.py:47
  192.1 10.0 %collective-permute-start = (bf16[2,2,128,512]{3,2,1,0:T(8,128)(2,1)}, bf16[2,2,128,512]{3,2,1,0:T(8,128)(2,1)}, u32[]{:S(2)}, u32[]{:S(2)}) collective-permute-start(bf16[2,2,128,512]{3,2,1,0:T(8,128)(2,1)} %bitcast.168), channel_id=1, source_target_pairs={{0,4},{4,8},{8,12},{12,16},{16,20},{20,24},{24,28},{1,5},{5,9},{9,... | collective-permute-start | bytes 1572872 | tf_op jit(solution)/shard_map/while/body/eval_jaxpr/ppermute | solution.py:16
  204.8 46.4 %copy-start.3 = (bf16[1,2,128,512]{3,2,1,0:T(8,128)(2,1)S(1)}, bf16[1,2,128,512]{3,2,1,0:T(8,128)(2,1)}, u32[]{:S(2)}) copy-start(bf16[1,2,128,512]{3,2,1,0:T(8,128)(2,1)} %get-tuple-element.113) | copy-start | bytes 786436 | tf_op jit(solution)/shard_map/while
  251.2 3.5 copy-start.1
  255.6 60.2 %all-gather.5.cloned.1.call-start = ((), (), s32[]{:S(2)}) async-start(), calls=%async_computation.1 | async-start | bytes 2621440 | tf_op jit(solution)/shard_map/while/body/eval_jaxpr/all_gather | solution.py:47
  256.7 10.0 %collective-permute-start = (bf16[2,2,128,512]{3,2,1,0:T(8,128)(2,1)}, bf16[2,2,128,512]{3,2,1,0:T(8,128)(2,1)}, u32[]{:S(2)}, u32[]{:S(2)}) collective-permute-start(bf16[2,2,128,512]{3,2,1,0:T(8,128)(2,1)} %bitcast.168), channel_id=1, source_target_pairs={{0,4},{4,8},{8,12},{12,16},{16,20},{20,24},{24,28},{1,5},{5,9},{9,... | collective-permute-start | bytes 1572872 | tf_op jit(solution)/shard_map/while/body/eval_jaxpr/ppermute | solution.py:16
  269.4 46.4 %copy-start.3 = (bf16[1,2,128,512]{3,2,1,0:T(8,128)(2,1)S(1)}, bf16[1,2,128,512]{3,2,1,0:T(8,128)(2,1)}, u32[]{:S(2)}) copy-start(bf16[1,2,128,512]{3,2,1,0:T(8,128)(2,1)} %get-tuple-element.113) | copy-start | bytes 786436 | tf_op jit(solution)/shard_map/while
  315.8 3.5 copy-start.1
  320.2 60.2 %all-gather.5.cloned.1.call-start = ((), (), s32[]{:S(2)}) async-start(), calls=%async_computation.1 | async-start | bytes 2621440 | tf_op jit(solution)/shard_map/while/body/eval_jaxpr/all_gather | solution.py:47
  321.3 10.0 %collective-permute-start = (bf16[2,2,128,512]{3,2,1,0:T(8,128)(2,1)}, bf16[2,2,128,512]{3,2,1,0:T(8,128)(2,1)}, u32[]{:S(2)}, u32[]{:S(2)}) collective-permute-start(bf16[2,2,128,512]{3,2,1,0:T(8,128)(2,1)} %bitcast.168), channel_id=1, source_target_pairs={{0,4},{4,8},{8,12},{12,16},{16,20},{20,24},{24,28},{1,5},{5,9},{9,... | collective-permute-start | bytes 1572872 | tf_op jit(solution)/shard_map/while/body/eval_jaxpr/ppermute | solution.py:16
  334.0 46.4 %copy-start.3 = (bf16[1,2,128,512]{3,2,1,0:T(8,128)(2,1)S(1)}, bf16[1,2,128,512]{3,2,1,0:T(8,128)(2,1)}, u32[]{:S(2)}) copy-start(bf16[1,2,128,512]{3,2,1,0:T(8,128)(2,1)} %get-tuple-element.113) | copy-start | bytes 786436 | tf_op jit(solution)/shard_map/while
  380.4 3.5 copy-start.1
  384.8 60.2 %all-gather.5.cloned.1.call-start = ((), (), s32[]{:S(2)}) async-start(), calls=%async_computation.1 | async-start | bytes 2621440 | tf_op jit(solution)/shard_map/while/body/eval_jaxpr/all_gather | solution.py:47
  385.9 10.0 %collective-permute-start = (bf16[2,2,128,512]{3,2,1,0:T(8,128)(2,1)}, bf16[2,2,128,512]{3,2,1,0:T(8,128)(2,1)}, u32[]{:S(2)}, u32[]{:S(2)}) collective-permute-start(bf16[2,2,128,512]{3,2,1,0:T(8,128)(2,1)} %bitcast.168), channel_id=1, source_target_pairs={{0,4},{4,8},{8,12},{12,16},{16,20},{20,24},{24,28},{1,5},{5,9},{9,... | collective-permute-start | bytes 1572872 | tf_op jit(solution)/shard_map/while/body/eval_jaxpr/ppermute | solution.py:16
  398.6 46.4 %copy-start.3 = (bf16[1,2,128,512]{3,2,1,0:T(8,128)(2,1)S(1)}, bf16[1,2,128,512]{3,2,1,0:T(8,128)(2,1)}, u32[]{:S(2)}) copy-start(bf16[1,2,128,512]{3,2,1,0:T(8,128)(2,1)} %get-tuple-element.113) | copy-start | bytes 786436 | tf_op jit(solution)/shard_map/while
  445.0 3.5 copy-start.1
  449.4 60.2 %all-gather.5.cloned.1.call-start = ((), (), s32[]{:S(2)}) async-start(), calls=%async_computation.1 | async-start | bytes 2621440 | tf_op jit(solution)/shard_map/while/body/eval_jaxpr/all_gather | solution.py:47
  450.5 10.0 %collective-permute-start = (bf16[2,2,128,512]{3,2,1,0:T(8,128)(2,1)}, bf16[2,2,128,512]{3,2,1,0:T(8,128)(2,1)}, u32[]{:S(2)}, u32[]{:S(2)}) collective-permute-start(bf16[2,2,128,512]{3,2,1,0:T(8,128)(2,1)} %bitcast.168), channel_id=1, source_target_pairs={{0,4},{4,8},{8,12},{12,16},{16,20},{20,24},{24,28},{1,5},{5,9},{9,... | collective-permute-start | bytes 1572872 | tf_op jit(solution)/shard_map/while/body/eval_jaxpr/ppermute | solution.py:16
  463.2 46.4 %copy-start.3 = (bf16[1,2,128,512]{3,2,1,0:T(8,128)(2,1)S(1)}, bf16[1,2,128,512]{3,2,1,0:T(8,128)(2,1)}, u32[]{:S(2)}) copy-start(bf16[1,2,128,512]{3,2,1,0:T(8,128)(2,1)} %get-tuple-element.113) | copy-start | bytes 786436 | tf_op jit(solution)/shard_map/while
  509.6 3.5 copy-start.1
  514.4 26.9 %copy-start.6 = (f32[2,1,2,128,512]{4,3,2,1,0:T(8,128)}, f32[2,1,2,128,512]{4,3,2,1,0:T(8,128)S(1)}, u32[]{:S(2)}) copy-start(f32[2,1,2,128,512]{4,3,2,1,0:T(8,128)S(1)} %copy.26) | copy-start | bytes 3145732
  514.4 20.0 %copy-start.8 = (f32[1,128,512]{2,1,0:T(8,128)S(1)}, f32[1,128,512]{2,1,0:T(8,128)}, u32[]{:S(2)}) copy-start(f32[1,128,512]{2,1,0:T(8,128)} %param.8) | copy-start | bytes 786436
  514.5 11.8 %collective-permute-start.1 = (bf16[2,1,2,128,512]{4,3,2,1,0:T(8,128)(2,1)S(1)}, bf16[2,1,2,128,512]{4,3,2,1,0:T(8,128)(2,1)S(1)}, u32[]{:S(2)}, u32[]{:S(2)}) collective-permute-start(bf16[2,1,2,128,512]{4,3,2,1,0:T(8,128)(2,1)S(1)} %convert_element_type.40), channel_id=1, source_target_pairs={{0,4},{4,8},{8,12},{12,16},{16,20},{20,24},{24,28},{1,5},{5,9},{9,... | collective-permute-start | bytes 1572872 | tf_op jit(solution)/shard_map/ppermute | solution.py:27
  518.2 10.8 %collective-permute-start.2 = (bf16[2,1,2,128,512]{4,3,2,1,0:T(8,128)(2,1)S(1)}, bf16[2,1,2,128,512]{4,3,2,1,0:T(8,128)(2,1)S(1)}, u32[]{:S(2)}, u32[]{:S(2)}) collective-permute-start(bf16[2,1,2,128,512]{4,3,2,1,0:T(8,128)(2,1)S(1)} %convert_element_type.40), channel_id=1, source_target_pairs={{4,0},{8,4},{12,8},{16,12},{20,16},{24,20},{28,24},{5,1},{9,5},{13... | collective-permute-start | bytes 1572872 | tf_op jit(solution)/shard_map/ppermute | solution.py:29
  529.1 5.3 collective-permute-start.3
  530.4 4.9 collective-permute-start.4
  541.3 1.2 copy-start.5
Sparse Core Ops, SparseCore 0:
  13.0 44.3 all-gather.2
  76.8 45.2 all-gather.4
  141.4 45.2 all-gather.4
  206.0 45.2 all-gather.4
  270.6 45.2 all-gather.4
  335.1 45.2 all-gather.4
  399.7 45.2 all-gather.4
  464.3 45.2 all-gather.4
where the time goes:
time: 558 us; the launch traced here: 551 us
  waiting for transfers between devices  414 us (74%)
  matrix products  44.8 us (8%)
  starting transfers between devices  36.5 us (7%)
  other arithmetic  24.7 us (4%)
  local copies, waits for them, and re-layouts  15 us (3%)
  between operations  14.9 us (3%)
    all_gather x8, waiting for transfers between devices, cross_fold(): gathered = lax.all_gather(mixed, 'cross', axis=2, tiled=True)  362 us
    ppermute x7, waiting for transfers between devices, passed_along(): return lax.ppermute(shard, axis, pairs)  42.6 us
    ppermute x7, starting transfers between devices, passed_along(): return lax.ppermute(shard, axis, pairs)  25.2 us
    dot_general x8, matrix products, cross_fold(): jnp.einsum('yk,rkx->ryx', coupling_rows[0], gathered[0], preferred_elemen...  14.4 us
    dot_general x8, matrix products, cross_fold(): jnp.einsum('yk,rkx->ryx', coupling_rows[0], gathered[1], preferred_elemen...  13.2 us
  transfers between devices with their start and end apart: 19, of which 18 were waited for; matrix products, arithmetic and copies ran while one was open for 0% of the time, Pallas kernels for 0%

commit v1 on v0

v1 whole, which is shorter than its diff:
```python
import functools

import jax
import jax.numpy as jnp
from jax import lax
from jax.experimental import pallas as pl
from jax.experimental.pallas import tpu as pltpu
from jax.sharding import PartitionSpec as P

MESH = pl.DeviceIdType.MESH
SIGMA_TOP = 2.0
CENTER = 128.0 / 30.0
FACE = 14.0 / 30.0
EDGE = 3.0 / 30.0
CORNER = 1.0 / 30.0
PAD = 16
RHS = 2
BF = jnp.bfloat16


def kernel(
    n_s, n_c,
    rhs_ref, slow_ref, depth_ref, line_ref, cross_ref,
    sol_ref, res_ref,
    rhs_full, c_full, src, mixed, s_in, o_buf, ext, p_out, p_in,
    c_send, c_recv, r_send, r_recv, s_send, s_recv, y_send, e_send, e_recv, p_send, p_recv,
):
    rows, cols = slow_ref.shape[1], slow_ref.shape[2]
    height = rows * n_c
    group = n_c // RHS
    width = cols // group
    chunk = min(128, height)
    chunks = height // chunk
    sec = lax.axis_index("sec")
    p = lax.axis_index("cross")
    r = p // group
    h = p % group
    odd = sec % 2

    def remote(source, target, send, recv, where):
        return pltpu.make_async_remote_copy(
            src_ref=source, dst_ref=target, send_sem=send, recv_sem=recv,
            device_id=where, device_id_type=MESH,
        )

    def at_sec(s):
        return {"sec": s, "cross": p}

    def at_cross(q):
        return {"sec": sec, "cross": q}

    barrier = pltpu.get_barrier_semaphore()
    for d in range(1, n_c):
        pl.semaphore_signal(barrier, inc=1, device_id=at_cross((p + d) % n_c), device_id_type=MESH)

    @pl.when(sec > 0)
    def _():
        pl.semaphore_signal(barrier, inc=1, device_id=at_sec(sec - 1), device_id_type=MESH)

    @pl.when(sec < n_s - 1)
    def _():
        pl.semaphore_signal(barrier, inc=1, device_id=at_sec(sec + 1), device_id_type=MESH)

    def block(q):
        return pl.ds(pl.multiple_of(q * rows, rows), rows)

    for b in range(RHS):
        for c in range(2):
            rhs_full[b, c, block(p), :] = rhs_ref[c, 0, b].astype(BF)
    for c in range(2):
        c_full[c, block(p), :] = cross_ref[0, c]
    zeros_pad = jnp.zeros((PAD, width), BF)
    for j in range(group):
        for c in range(2):
            o_buf[j, c, 0:PAD, :] = zeros_pad
            o_buf[j, c, PAD + height : PAD + height + PAD, :] = zeros_pad

    pl.semaphore_wait(barrier, n_c - 1 + jnp.minimum(sec, 1) + jnp.minimum(n_s - 1 - sec, 1))

    def c_copy(q, way, to):
        return remote(c_full.at[:, block(q), :], c_full.at[:, block(q), :], c_send.at[way, q], c_recv.at[q], at_cross(to))

    def r_copy(b, q, way, to):
        return remote(rhs_full.at[b, :, block(q), :], rhs_full.at[b, :, block(q), :], r_send.at[b, way, q], r_recv.at[b, q], at_cross(to))

    def moves_right(b):
        return p < n_c - 1 if b == 1 else p + 1 < group

    def moves_left(b):
        return p > 0 if b == 0 else p - 1 >= group

    last = n_c - 1
    for t in range(n_c):
        a = p - t
        a0 = jnp.maximum(a, 0)
        z = p + t
        z0 = jnp.minimum(z, last)
        right = jnp.minimum(p + 1, last)
        left = jnp.maximum(p - 1, 0)
        for b in (1, 0):
            if t > 0:
                got = (a >= 0) if b == 1 else jnp.logical_and(a >= 0, p < group)

                @pl.when(got)
                def _():
                    r_copy(b, a0, 0, left).wait_recv()

            @pl.when(jnp.logical_and(a >= 0, moves_right(b)))
            def _():
                r_copy(b, a0, 0, right).start()

        for b in (0, 1):
            if t > 0:
                got = (z <= last) if b == 0 else jnp.logical_and(z <= last, p >= group)

                @pl.when(got)
                def _():
                    r_copy(b, z0, 1, right).wait_recv()

            @pl.when(jnp.logical_and(z <= last, moves_left(b)))
            def _():
                r_copy(b, z0, 1, left).start()

        if t > 0:
            @pl.when(a >= 0)
            def _():
                c_copy(a0, 0, left).wait_recv()

        @pl.when(jnp.logical_and(a >= 0, p < last))
        def _():
            c_copy(a0, 0, right).start()

        if t > 0:
            @pl.when(z <= last)
            def _():
                c_copy(z0, 1, right).wait_recv()

        @pl.when(jnp.logical_and(z <= last, p > 0))
        def _():
            c_copy(z0, 1, left).start()

    lo = odd * h
    hi = lo + (1 - odd) * group + odd

    def lines(i):
        return pl.ds(pl.multiple_of(i * chunk, chunk), chunk)

    def padded_lines(i):
        return pl.ds(pl.multiple_of(PAD + i * chunk, PAD), chunk)

    def part(j):
        return pl.ds(pl.multiple_of(j * width, width), width)

    def s_copy(i, j):
        return remote(
            o_buf.at[j, :, padded_lines(i), :], s_in.at[j, :, lines(i), :], s_send.at[i, j], s_recv.at[i, j],
            at_sec(jnp.minimum(sec + 1, n_s - 1)),
        )

    def y_copy(i, d):
        other = r * group + (h + d) % group
        return remote(
            s_in.at[h, :, lines(i), :], s_in.at[h, :, lines(i), :], y_send.at[i, d], s_recv.at[i, h], at_cross(other)
        )

    def s_wait(i, j):
        remote(
            o_buf.at[0, :, padded_lines(i), :], s_in.at[j, :, lines(i), :], s_send.at[i, 0], s_recv.at[i, j],
            at_sec(jnp.maximum(sec - 1, 0)),
        ).wait_recv()

    def times(left, w0, w1):
        one = jnp.dot(left, w0, preferred_element_type=jnp.float32)
        two = jnp.dot(left, w1, preferred_element_type=jnp.float32)
        half = left.shape[0] // 2
        return one[:half] - two[half:], two[:half] + one[half:]

    def take(i, _):
        @pl.when(sec > 0)
        def _():
            s_wait(i, h)

            @pl.when(odd == 0)
            def _():
                for d in range(1, group):
                    y_copy(i, d).start()

            for d in range(1, group):
                s_wait(i, (h + d) % group)

            for c in range(2):
                for j in range(group):
                    at = slice(j * width, (j + 1) * width)
                    src[c, :, at] = (
                        rhs_full[r, c, lines(i), at].astype(jnp.float32) + s_in[j, c, lines(i), :].astype(jnp.float32)
                    ).astype(BF)

        @pl.when(sec == 0)
        def _():
            for c in range(2):
                src[c] = rhs_full[r, c, lines(i), :]

        left = src[...].reshape(2 * chunk, cols)

        def of_part(j, _):
            re, im = times(left, line_ref[0, 0, :, part(j)], line_ref[0, 1, :, part(j)])
            mixed[j, 0, lines(i), :] = re.astype(BF)
            mixed[j, 1, lines(i), :] = im.astype(BF)
            return 0

        lax.fori_loop(lo, hi, of_part, 0)
        return 0

    lax.fori_loop(0, chunks, take, 0)

    def give(i, _):
        left = c_full[:, lines(i), :].reshape(2 * chunk, height)

        def of_part(j, _):
            re, im = times(left, mixed[j, 0], mixed[j, 1])
            o_buf[j, 0, padded_lines(i), :] = re.astype(BF)
            o_buf[j, 1, padded_lines(i), :] = im.astype(BF)

            @pl.when(sec < n_s - 1)
            def _():
                s_copy(i, j).start()

            return 0

        lax.fori_loop(lo, hi, of_part, 0)
        return 0

    lax.fori_loop(0, chunks, give, 0)

    tall = rows + 2 * PAD

    def own(q):
        return pl.ds(pl.multiple_of(q * rows, PAD), tall)

    def e_copy(d):
        q = (p + d) % n_c
        return remote(o_buf.at[h, :, own(q), :], ext.at[p], e_send.at[d], e_recv.at[p], at_cross(q))

    for d in range(1, n_c):
        e_copy(d).start()
    ext[p] = o_buf[h, :, own(p), :]
    for d in range(1, n_c):
        q = (p + d) % n_c
        remote(o_buf.at[h, :, own(q), :], ext.at[q], e_send.at[d], e_recv.at[q], at_cross(q)).wait_recv()

    column = lax.broadcasted_iota(jnp.int32, (rows, cols), 1)

    def sideways(v):
        before = jnp.where(column == 0, 0.0, pltpu.roll(v, 1, 1))
        after = jnp.where(column == cols - 1, 0.0, pltpu.roll(v, cols - 1, 1))
        return before + after

    for b in range(RHS):
        for c in range(2):
            f = jnp.concatenate([ext[b * group + j, c].astype(jnp.float32) for j in range(group)], axis=1)
            here = f[PAD : PAD + rows]
            updown = (pltpu.roll(f, 1, 0) + pltpu.roll(f, tall - 1, 0))[PAD : PAD + rows]
            faces = updown + sideways(here)
            corners = sideways(updown)
            sol_ref[c, 0, b] = here
            p_out[c, b] = (FACE * here + EDGE * faces + CORNER * corners).astype(BF)
            res_ref[c, 0, b] = rhs_ref[c, 0, b] - CENTER * here + (FACE * faces + EDGE * corners)

    def p_copy(way):
        to = jnp.maximum(sec - 1, 0) if way == 1 else jnp.minimum(sec + 1, n_s - 1)
        return remote(p_out, p_in.at[way], p_send.at[way], p_recv.at[way], at_sec(to))

    @pl.when(sec < n_s - 1)
    def _():
        p_copy(0).start()

    @pl.when(sec > 0)
    def _():
        p_copy(1).start()

    line = lax.broadcasted_iota(jnp.int32, (1, cols), 1)
    distance = jnp.minimum(line, cols - 1 - line).astype(jnp.float32)
    depth = jnp.full((1, cols), depth_ref[0], jnp.int32).astype(jnp.float32)
    ramp = jnp.maximum(depth - distance, 0.0) / depth
    damping = SIGMA_TOP * ramp * ramp
    wave_real = slow_ref[0]
    wave_imag = wave_real * damping
    for b in range(RHS):
        re, im = sol_ref[0, 0, b], sol_ref[1, 0, b]
        res_ref[0, 0, b] += wave_real * re - wave_imag * im
        res_ref[1, 0, b] += wave_real * im + wave_imag * re

    def neighbour(way):
        p_copy(way).wait_recv()
        for b in range(RHS):
            for c in range(2):
                res_ref[c, 0, b] += p_in[way, c, b].astype(jnp.float32)

    @pl.when(sec > 0)
    def _():
        neighbour(0)

    @pl.when(sec < n_s - 1)
    def _():
        neighbour(1)

    for t in range(n_c):
        a = p - t
        a0 = jnp.maximum(a, 0)
        z = p + t
        z0 = jnp.minimum(z, last)
        right = jnp.minimum(p + 1, last)
        left = jnp.maximum(p - 1, 0)
        for b in range(RHS):
            @pl.when(jnp.logical_and(a >= 0, moves_right(b)))
            def _():
                r_copy(b, a0, 0, right).wait_send()

            @pl.when(jnp.logical_and(z <= last, moves_left(b)))
            def _():
                r_copy(b, z0, 1, left).wait_send()

        @pl.when(jnp.logical_and(a >= 0, p < last))
        def _():
            c_copy(a0, 0, right).wait_send()

        @pl.when(jnp.logical_and(z <= last, p > 0))
        def _():
            c_copy(z0, 1, left).wait_send()

    def sent(i, _):
        @pl.when(sec < n_s - 1)
        def _():
            def one(j, _):
                s_copy(i, j).wait_send()
                return 0

            lax.fori_loop(lo, hi, one, 0)

        @pl.when(jnp.logical_and(sec > 0, odd == 0))
        def _():
            for d in range(1, group):
                y_copy(i, d).wait_send()

        return 0

    lax.fori_loop(0, chunks, sent, 0)
    for d in range(1, n_c):
        e_copy(d).wait_send()

    @pl.when(sec < n_s - 1)
    def _():
        p_copy(0).wait_send()

    @pl.when(sec > 0)
    def _():
        p_copy(1).wait_send()


def per_device(n_s, n_c, rhs_field, slowness, absorb_depth, line_inverse, cross_inverse):
    rows, cols = slowness.shape[1:]
    height = rows * n_c
    group = n_c // RHS
    width = cols // group
    chunk = min(128, height)
    chunks = height // chunk
    vmem = pl.BlockSpec(memory_space=pltpu.VMEM)
    dma = pltpu.SemaphoreType.DMA
    out = jax.ShapeDtypeStruct(rhs_field.shape, jnp.float32)
    return pl.pallas_call(
        functools.partial(kernel, n_s, n_c),
        out_shape=(out, out),
        in_specs=[vmem, vmem, pl.BlockSpec(memory_space=pltpu.SMEM), vmem, vmem],
        out_specs=(vmem, vmem),
        scratch_shapes=[
            pltpu.VMEM((RHS, 2, height, cols), BF),
            pltpu.VMEM((2, height, height), BF),
            pltpu.VMEM((2, chunk, cols), BF),
            pltpu.VMEM((group, 2, height, width), BF),
            pltpu.VMEM((group, 2, height, width), BF),
            pltpu.VMEM((group, 2, height + 2 * PAD, width), BF),
            pltpu.VMEM((n_c, 2, rows + 2 * PAD, width), BF),
            pltpu.VMEM((2, RHS, rows, cols), BF),
            pltpu.VMEM((2, 2, RHS, rows, cols), BF),
            dma((2, n_c)), dma((n_c,)),
            dma((RHS, 2, n_c)), dma((RHS, n_c)),
            dma((chunks, group)), dma((chunks, group)), dma((chunks, group)),
            dma((n_c,)), dma((n_c,)),
            dma((2,)), dma((2,)),
        ],
        compiler_params=pltpu.CompilerParams(
            collective_id=0, has_side_effects=True, vmem_limit_bytes=56 * 1024 * 1024
        ),
        name="sweep",
    )(rhs_field, slowness, absorb_depth, line_inverse, cross_inverse)


def solution(mesh):
    field = P(None, "sec", None, "cross", None)
    return jax.shard_map(
        functools.partial(per_device, mesh.shape["sec"], mesh.shape["cross"]),
        mesh=mesh,
        in_specs=(
            field,
            P("sec", "cross", None),
            P("sec"),
            P("sec", None, None, None),
            P("sec", None, "cross", None),
        ),
        out_specs=(field, field),
        check_vma=False,
    )
```

time: 558 us -> 165 us (0.30); the launches traced: 551 us -> 164 us
  waiting for transfers between devices: 414 us -> 0 us
  Pallas kernels: 0 us -> 160 us
  matrix products: 44.8 us -> 0 us
  starting transfers between devices: 36.5 us -> 0 us
  other arithmetic: 24.7 us -> 0 us
  between operations: 14.9 us -> 1.29 us
  local copies, waits for them, and re-layouts: 15 us -> 3.32 us
    all_gather x8 -> x0, waiting for transfers between devices: 362 us -> none  [cross_fold(): gathered = lax.all_gather(mixed, 'cross', axis=2, tiled=True)]
    pallas_call x0 -> x1, Pallas kernels: none -> 160 us  [per_device(): pl.pallas_call(functools.partial(kernel, n_s, n_c), out_shape=(out, out),...]
    ppermute x11 -> x0, waiting for transfers between devices: 51.6 us -> none  [the longest x7 42.6 us: passed_along(): return lax.ppermute(shard, axis, pairs)]
    dot_general x64 -> x0, matrix products: 44.8 us -> none  [the longest x8 14.4 us: cross_fold(): jnp.einsum('yk,rkx->ryx', coupling_rows[0], gathered[0], preferred_elemen...]
    ppermute x11 -> x0, starting transfers between devices: 36.1 us -> none  [the longest x7 25.2 us: passed_along(): return lax.ppermute(shard, axis, pairs)]
    another operation x30 -> x0, local copies, waits for them, and re-layouts: 13 us -> none
    convert_element_type x10 -> x0, other arithmetic: 10.4 us -> none  [the longest x8 9.79 us: sweep_section(): source = (rhs_local[:, 0] + prior).astype(jnp.bfloat16)]
    another operation x16 -> x0, other arithmetic: 7.33 us -> none  [the longest x8 6.77 us: complex_line(): return jnp.stack([real_part, imag_part]).astype(jnp.bfloat16)]
  transfers between devices with their start and end apart: 19 -> 0, of which waited for: 18 -> 0; matrix products, arithmetic and copies ran while one was open for 0% -> 0% of each run, Pallas kernels for 0% -> 0%
where the time goes in v1:
time: 165 us; the launch traced here: 164 us
  Pallas kernels  160 us (97%)
  local copies, waits for them, and re-layouts  3.32 us (2%)
    pallas_call x1, Pallas kernels, per_device(): pl.pallas_call(functools.partial(kernel, n_s, n_c), out_shape=(out, out),...  160 us
    unnamed x4, local copies, waits for them, and re-layouts  3.32 us

profile of v1, /device:TPU:29, one launch (start us, length us, event | category | flops | bytes accessed | tf_op | source)
XLA Modules:
  0.0 164.4 jit_solution(4671049172677349189)
XLA Ops:
  1.3 159.8 %sweep.1 = (f32[2,1,2,128,512]{4,3,2,1,0:T(8,128)}, f32[2,1,2,128,512]{4,3,2,1,0:T(8,128)}) custom-call(f32[2,1,2,128,512]{4,3,2,1,0:T(8,128)} %rhs_ref.1, f32[1,128,512]{2,1,0:T(8,128)} %slow_ref.1, s32[1]{0:T(128)S(6)} %copy.9.depth_ref, bf16[1,2,512,512]{3,2,1,0:T(8,128)(2,1)} %line_ref.1, bf16[1,2,128,512]{3,2,1,0:T(8,128)(2,1)} %cross_ref.1), custom_call_target="tpu_custom_call" | custom-call | tf_op jit(solution)/shard_map/sweep/pallas_call | solution.py:370
  161.1 0.0 copy-start
  161.1 2.4 %copy.10 = f32[2,1,2,128,512]{4,3,2,1,0:T(8,128)} copy(f32[2,1,2,128,512]{4,3,2,1,0:T(8,128)} %get-tuple-element.4) | data formatting | bytes 2097152
  163.4 0.0 copy-done
  163.4 1.0 copy.11
Async XLA Ops:
  161.1 2.4 %copy-start = (f32[2,1,2,128,512]{4,3,2,1,0:T(8,128)S(1)}, f32[2,1,2,128,512]{4,3,2,1,0:T(8,128)}, u32[]{:S(2)}) copy-start(f32[2,1,2,128,512]{4,3,2,1,0:T(8,128)} %get-tuple-element.5) | copy-start | bytes 3145732

commit v2 on v1

--- a/solution.py
+++ b/solution.py
@@ -22,8 +22,9 @@
     n_s, n_c,
     rhs_ref, slow_ref, depth_ref, line_ref, cross_ref,
     sol_ref, res_ref,
-    rhs_full, c_full, src, mixed, s_in, o_buf, ext, p_out, p_in,
-    c_send, c_recv, r_send, r_recv, s_send, s_recv, y_send, e_send, e_recv, p_send, p_recv,
+    rhs_full, c_full, r_in, c_in, l_in, weight, direct, src, mixed, s_in, o_buf, ext, p_out, p_in,
+    c_send, c_recv, r_send, r_recv, f_send, f_recv, l_send, l_recv,
+    s_send, s_recv, y_send, d_send, e_send, e_recv, p_send, p_recv,
 ):
     rows, cols = slow_ref.shape[1], slow_ref.shape[2]
     height = rows * n_c
@@ -61,6 +62,14 @@
     def _():
         pl.semaphore_signal(barrier, inc=1, device_id=at_sec(sec + 1), device_id_type=MESH)
 
+    @pl.when(jnp.logical_and(odd == 1, sec >= 2))
+    def _():
+        pl.semaphore_signal(barrier, inc=1, device_id=at_sec(sec - 2), device_id_type=MESH)
+
+    @pl.when(jnp.logical_and(odd == 1, sec <= n_s - 3))
+    def _():
+        pl.semaphore_signal(barrier, inc=1, device_id=at_sec(sec + 2), device_id_type=MESH)
+
     def block(q):
         return pl.ds(pl.multiple_of(q * rows, rows), rows)
 
@@ -75,13 +84,65 @@
             o_buf[j, c, 0:PAD, :] = zeros_pad
             o_buf[j, c, PAD + height : PAD + height + PAD, :] = zeros_pad
 
-    pl.semaphore_wait(barrier, n_c - 1 + jnp.minimum(sec, 1) + jnp.minimum(n_s - 1 - sec, 1))
+    nearest = jnp.minimum(sec, 1) + jnp.minimum(n_s - 1 - sec, 1)
+    second = jnp.minimum(sec // 2, 1) + jnp.minimum((n_s - 1 - sec) // 2, 1)
+    pl.semaphore_wait(barrier, n_c - 1 + nearest + odd * second)
 
     def c_copy(q, way, to):
         return remote(c_full.at[:, block(q), :], c_full.at[:, block(q), :], c_send.at[way, q], c_recv.at[q], at_cross(to))
 
     def r_copy(b, q, way, to):
         return remote(rhs_full.at[b, :, block(q), :], rhs_full.at[b, :, block(q), :], r_send.at[b, way, q], r_recv.at[b, q], at_cross(to))
+
+    partner = sec + 1 - 2 * odd
+
+    def f_copy(kind, q):
+        source, target = (rhs_full.at[r], r_in) if kind == 0 else (c_full, c_in)
+        return remote(
+            source.at[:, block(q), :], target.at[:, block(q), :], f_send.at[kind, q], f_recv.at[kind, q], at_sec(partner)
+        )
+
+    def l_copy():
+        return remote(line_ref.at[0], l_in, l_send, l_recv, at_sec(partner))
+
+    def times(left, w0, w1):
+        one = jnp.dot(left, w0, preferred_element_type=jnp.float32)
+        two = jnp.dot(left, w1, preferred_element_type=jnp.float32)
+        half = left.shape[0] // 2
+        return one[:half] - two[half:], two[:half] + one[half:]
+
+    def lines(i):
+        return pl.ds(pl.multiple_of(i * chunk, chunk), chunk)
+
+    def part(j):
+        return pl.ds(pl.multiple_of(j * width, width), width)
+
+    span = min(128, cols)
+
+    def weights():
+        @pl.when(odd == 0)
+        def _():
+            for c in range(2):
+                weight[c] = line_ref[0, c, :, part(h)]
+
+        @pl.when(odd == 1)
+        def _():
+            l_copy().wait_recv()
+
+            def rows_of(i, _):
+                at = pl.ds(pl.multiple_of(i * span, span), span)
+                re, im = times(
+                    l_in[:, at, :].reshape(2 * span, cols), line_ref[0, 0, :, part(h)], line_ref[0, 1, :, part(h)]
+                )
+                weight[0, at, :] = re.astype(BF)
+                weight[1, at, :] = im.astype(BF)
+                return 0
+
+            lax.fori_loop(0, cols // span, rows_of, 0)
+
+    @pl.when(odd == 0)
+    def _():
+        l_copy().start()
 
     def moves_right(b):
         return p < n_c - 1 if b == 1 else p + 1 < group
@@ -105,6 +166,10 @@
                 def _():
                     r_copy(b, a0, 0, left).wait_recv()
 
+                @pl.when(jnp.logical_and(got, jnp.logical_and(odd == 0, r == b)))
+                def _():
+                    f_copy(0, a0).start()
+
             @pl.when(jnp.logical_and(a >= 0, moves_right(b)))
             def _():
                 r_copy(b, a0, 0, right).start()
@@ -117,6 +182,10 @@
                 def _():
                     r_copy(b, z0, 1, right).wait_recv()
 
+                @pl.when(jnp.logical_and(got, jnp.logical_and(odd == 0, r == b)))
+                def _():
+                    f_copy(0, z0).start()
+
             @pl.when(jnp.logical_and(z <= last, moves_left(b)))
             def _():
                 r_copy(b, z0, 1, left).start()
@@ -126,6 +195,10 @@
             def _():
                 c_copy(a0, 0, left).wait_recv()
 
+            @pl.when(jnp.logical_and(a >= 0, odd == 0))
+            def _():
+                f_copy(1, a0).start()
+
         @pl.when(jnp.logical_and(a >= 0, p < last))
         def _():
             c_copy(a0, 0, right).start()
@@ -135,26 +208,29 @@
             def _():
                 c_copy(z0, 1, right).wait_recv()
 
+            @pl.when(jnp.logical_and(z <= last, odd == 0))
+            def _():
+                f_copy(1, z0).start()
+
         @pl.when(jnp.logical_and(z <= last, p > 0))
         def _():
             c_copy(z0, 1, left).start()
 
-    lo = odd * h
-    hi = lo + (1 - odd) * group + odd
-
-    def lines(i):
-        return pl.ds(pl.multiple_of(i * chunk, chunk), chunk)
+        if t == 0:
+            @pl.when(odd == 0)
+            def _():
+                f_copy(0, p).start()
+                f_copy(1, p).start()
+
+            weights()
 
     def padded_lines(i):
         return pl.ds(pl.multiple_of(PAD + i * chunk, PAD), chunk)
 
-    def part(j):
-        return pl.ds(pl.multiple_of(j * width, width), width)
-
-    def s_copy(i, j):
+    def s_copy(i):
         return remote(
-            o_buf.at[j, :, padded_lines(i), :], s_in.at[j, :, lines(i), :], s_send.at[i, j], s_recv.at[i, j],
-            at_sec(jnp.minimum(sec + 1, n_s - 1)),
+            o_buf.at[h, :, padded_lines(i), :], s_in.at[h, :, lines(i), :], s_send.at[i], s_recv.at[i, h],
+            at_sec(jnp.minimum(sec + 2, n_s - 1)),
         )
 
     def y_copy(i, d):
@@ -163,71 +239,90 @@
             s_in.at[h, :, lines(i), :], s_in.at[h, :, lines(i), :], y_send.at[i, d], s_recv.at[i, h], at_cross(other)
         )
 
-    def s_wait(i, j):
-        remote(
-            o_buf.at[0, :, padded_lines(i), :], s_in.at[j, :, lines(i), :], s_send.at[i, 0], s_recv.at[i, j],
-            at_sec(jnp.maximum(sec - 1, 0)),
-        ).wait_recv()
-
-    def times(left, w0, w1):
-        one = jnp.dot(left, w0, preferred_element_type=jnp.float32)
-        two = jnp.dot(left, w1, preferred_element_type=jnp.float32)
-        half = left.shape[0] // 2
-        return one[:half] - two[half:], two[:half] + one[half:]
+    def d_copy(i, j):
+        return remote(
+            s_in.at[j, :, lines(i), :], s_in.at[j, :, lines(i), :], d_send.at[i, j], s_recv.at[i, j], at_sec(partner)
+        )
+
+    @pl.when(odd == 1)
+    def _():
+        def own_lines(i, _):
+            re, im = times(
+                rhs_full[r, :, lines(i), :].reshape(2 * chunk, cols), line_ref[0, 0, :, part(h)], line_ref[0, 1, :, part(h)]
+            )
+            direct[0, lines(i), :] = re
+            direct[1, lines(i), :] = im
+            return 0
+
+        lax.fori_loop(0, chunks, own_lines, 0)
+        for q in range(n_c):
+            f_copy(0, q).wait_recv()
+
+    @pl.when(odd == 0)
+    def _():
+        r_in[...] = rhs_full[r]
 
     def take(i, _):
-        @pl.when(sec > 0)
-        def _():
-            s_wait(i, h)
-
-            @pl.when(odd == 0)
+        @pl.when(sec >= 2)
+        def _():
+            d_copy(i, h).wait_recv()
+
+            @pl.when(odd == 1)
             def _():
                 for d in range(1, group):
                     y_copy(i, d).start()
+                d_copy(i, h).start()
 
             for d in range(1, group):
-                s_wait(i, (h + d) % group)
+                j = (h + d) % group
+                d_copy(i, j).wait_recv()
+
+                @pl.when(odd == 1)
+                def _():
+                    d_copy(i, j).start()
 
             for c in range(2):
                 for j in range(group):
                     at = slice(j * width, (j + 1) * width)
                     src[c, :, at] = (
-                        rhs_full[r, c, lines(i), at].astype(jnp.float32) + s_in[j, c, lines(i), :].astype(jnp.float32)
+                        r_in[c, lines(i), at].astype(jnp.float32) + s_in[j, c, lines(i), :].astype(jnp.float32)
                     ).astype(BF)
 
-        @pl.when(sec == 0)
-        def _():
-            for c in range(2):
-                src[c] = rhs_full[r, c, lines(i), :]
-
-        left = src[...].reshape(2 * chunk, cols)
-
-        def of_part(j, _):
-            re, im = times(left, line_ref[0, 0, :, part(j)], line_ref[0, 1, :, part(j)])
-            mixed[j, 0, lines(i), :] = re.astype(BF)
-            mixed[j, 1, lines(i), :] = im.astype(BF)
+        @pl.when(sec < 2)
+        def _():
+            src[...] = r_in[:, lines(i), :]
+
+        re, im = times(src[...].reshape(2 * chunk, cols), weight[0], weight[1])
+        mixed[odd, 0, lines(i), :] = re.astype(BF)
+        mixed[odd, 1, lines(i), :] = im.astype(BF)
+        return 0
+
+    lax.fori_loop(0, chunks, take, 0)
+
+    @pl.when(odd == 1)
+    def _():
+        for q in range(n_c):
+            f_copy(1, q).wait_recv()
+
+        def even_layer(i, _):
+            re, im = times(c_in[:, lines(i), :].reshape(2 * chunk, height), mixed[1, 0], mixed[1, 1])
+            mixed[0, 0, lines(i), :] = (direct[0, lines(i), :] + re).astype(BF)
+            mixed[0, 1, lines(i), :] = (direct[1, lines(i), :] + im).astype(BF)
             return 0
 
-        lax.fori_loop(lo, hi, of_part, 0)
-        return 0
-
-    lax.fori_loop(0, chunks, take, 0)
+        lax.fori_loop(0, chunks, even_layer, 0)
+
+    hands_on = jnp.logical_and(odd == 1, sec <= n_s - 3)
 
     def give(i, _):
-        left = c_full[:, lines(i), :].reshape(2 * chunk, height)
-
-        def of_part(j, _):
-            re, im = times(left, mixed[j, 0], mixed[j, 1])
-            o_buf[j, 0, padded_lines(i), :] = re.astype(BF)
-            o_buf[j, 1, padded_lines(i), :] = im.astype(BF)
-
-            @pl.when(sec < n_s - 1)
-            def _():
-                s_copy(i, j).start()
-
-            return 0
-
-        lax.fori_loop(lo, hi, of_part, 0)
+        re, im = times(c_full[:, lines(i), :].reshape(2 * chunk, height), mixed[0, 0], mixed[0, 1])
+        o_buf[h, 0, padded_lines(i), :] = re.astype(BF)
+        o_buf[h, 1, padded_lines(i), :] = im.astype(BF)
+
+        @pl.when(hands_on)
+        def _():
+            s_copy(i).start()
+
         return 0
 
     lax.fori_loop(0, chunks, give, 0)
@@ -329,20 +424,25 @@
             c_copy(z0, 1, left).wait_send()
 
     def sent(i, _):
-        @pl.when(sec < n_s - 1)
-        def _():
-            def one(j, _):
-                s_copy(i, j).wait_send()
-                return 0
-
-            lax.fori_loop(lo, hi, one, 0)
-
-        @pl.when(jnp.logical_and(sec > 0, odd == 0))
+        @pl.when(hands_on)
+        def _():
+            s_copy(i).wait_send()
+
+        @pl.when(jnp.logical_and(sec >= 2, odd == 1))
         def _():
             for d in range(1, group):
                 y_copy(i, d).wait_send()
+            for j in range(group):
+                d_copy(i, j).wait_send()
 
         return 0
+
+    @pl.when(odd == 0)
+    def _():
+        l_copy().wait_send()
+        for q in range(n_c):
+            f_copy(0, q).wait_send()
+            f_copy(1, q).wait_send()
 
     lax.fori_loop(0, chunks, sent, 0)
     for d in range(1, n_c):
@@ -375,8 +475,13 @@
         scratch_shapes=[
             pltpu.VMEM((RHS, 2, height, cols), BF),
             pltpu.VMEM((2, height, height), BF),
+            pltpu.VMEM((2, height, cols), BF),
+            pltpu.VMEM((2, height, height), BF),
+            pltpu.VMEM((2, cols, cols), BF),
+            pltpu.VMEM((2, cols, width), BF),
+            pltpu.VMEM((2, height, width), jnp.float32),
             pltpu.VMEM((2, chunk, cols), BF),
-            pltpu.VMEM((group, 2, height, width), BF),
+            pltpu.VMEM((2, 2, height, width), BF),
             pltpu.VMEM((group, 2, height, width), BF),
             pltpu.VMEM((group, 2, height + 2 * PAD, width), BF),
             pltpu.VMEM((n_c, 2, rows + 2 * PAD, width), BF),
@@ -384,7 +489,8 @@
             pltpu.VMEM((2, 2, RHS, rows, cols), BF),
             dma((2, n_c)), dma((n_c,)),
             dma((RHS, 2, n_c)), dma((RHS, n_c)),
-            dma((chunks, group)), dma((chunks, group)), dma((chunks, group)),
+            dma((2, n_c)), dma((2, n_c)), dma, dma,
+            dma((chunks,)), dma((chunks, group)), dma((chunks, group)), dma((chunks, group)),
             dma((n_c,)), dma((n_c,)),
             dma((2,)), dma((2,)),
         ],

time: 165 us -> 142 us (0.86)
  Pallas kernels: 160 us -> 137 us
    pallas_call x1, Pallas kernels: 160 us -> 137 us  [per_device(): pl.pallas_call(functools.partial(kernel, n_s, n_c), out_shape=(out, out),...]
where the time goes in v2:
time: 142 us
  Pallas kernels  137 us (96%)
  local copies, waits for them, and re-layouts  3.32 us (2%)
    pallas_call x1, Pallas kernels, per_device(): pl.pallas_call(functools.partial(kernel, n_s, n_c), out_shape=(out, out),...  137 us
    unnamed x4, local copies, waits for them, and re-layouts  3.32 us

profile of v2, /device:TPU:29, one launch (start us, length us, event | category | flops | bytes accessed | tf_op | source)
XLA Modules:
  0.0 141.5 jit_solution(10601442073689773453)
XLA Ops:
  1.3 136.9 %sweep.1 = (f32[2,1,2,128,512]{4,3,2,1,0:T(8,128)}, f32[2,1,2,128,512]{4,3,2,1,0:T(8,128)}) custom-call(f32[2,1,2,128,512]{4,3,2,1,0:T(8,128)} %rhs_ref.1, f32[1,128,512]{2,1,0:T(8,128)} %slow_ref.1, s32[1]{0:T(128)S(6)} %copy.9.depth_ref, bf16[1,2,512,512]{3,2,1,0:T(8,128)(2,1)} %line_ref.1, bf16[1,2,128,512]{3,2,1,0:T(8,128)(2,1)} %cross_ref.1), custom_call_target="tpu_custom_call" | custom-call | tf_op jit(solution)/shard_map/sweep/pallas_call | solution.py:470
  138.2 0.0 copy-start
  138.2 2.4 %copy.10 = f32[2,1,2,128,512]{4,3,2,1,0:T(8,128)} copy(f32[2,1,2,128,512]{4,3,2,1,0:T(8,128)} %get-tuple-element.4) | data formatting | bytes 2097152
  140.6 0.0 copy-done
  140.6 1.0 copy.11
Async XLA Ops:
  138.2 2.4 %copy-start = (f32[2,1,2,128,512]{4,3,2,1,0:T(8,128)S(1)}, f32[2,1,2,128,512]{4,3,2,1,0:T(8,128)}, u32[]{:S(2)}) copy-start(f32[2,1,2,128,512]{4,3,2,1,0:T(8,128)} %get-tuple-element.5) | copy-start | bytes 3145732

commit v3 on v2

--- a/solution.py
+++ b/solution.py
@@ -22,7 +22,7 @@
     n_s, n_c,
     rhs_ref, slow_ref, depth_ref, line_ref, cross_ref,
     sol_ref, res_ref,
-    rhs_full, c_full, r_in, c_in, l_in, weight, direct, src, mixed, s_in, o_buf, ext, p_out, p_in,
+    rhs_full, c_full, r_in, c_in, l_in, weight, direct, src, both, mixed, s_in, o_buf, ext, p_out, p_in,
     c_send, c_recv, r_send, r_recv, f_send, f_recv, l_send, l_recv,
     s_send, s_recv, y_send, d_send, e_send, e_recv, p_send, p_recv,
 ):
@@ -151,78 +151,115 @@
         return p > 0 if b == 0 else p - 1 >= group
 
     last = n_c - 1
-    for t in range(n_c):
-        a = p - t
-        a0 = jnp.maximum(a, 0)
-        z = p + t
-        z0 = jnp.minimum(z, last)
-        right = jnp.minimum(p + 1, last)
-        left = jnp.maximum(p - 1, 0)
+    right = jnp.minimum(p + 1, last)
+    left = jnp.maximum(p - 1, 0)
+
+    def places(t):
+        return p - t >= 0, jnp.maximum(p - t, 0), p + t <= last, jnp.minimum(p + t, last)
+
+    def forward(kind, q, got):
+        @pl.when(jnp.logical_and(got, odd == 0))
+        def _():
+            f_copy(kind, q).start()
+
+    def relay_r(t):
+        is_a, a, is_z, z = places(t)
         for b in (1, 0):
             if t > 0:
-                got = (a >= 0) if b == 1 else jnp.logical_and(a >= 0, p < group)
+                got = is_a if b == 1 else jnp.logical_and(is_a, p < group)
 
                 @pl.when(got)
                 def _():
-                    r_copy(b, a0, 0, left).wait_recv()
-
-                @pl.when(jnp.logical_and(got, jnp.logical_and(odd == 0, r == b)))
-                def _():
-                    f_copy(0, a0).start()
-
-            @pl.when(jnp.logical_and(a >= 0, moves_right(b)))
-            def _():
-                r_copy(b, a0, 0, right).start()
+                    r_copy(b, a, 0, left).wait_recv()
+
+                forward(0, a, jnp.logical_and(got, r == b))
+
+            @pl.when(jnp.logical_and(is_a, moves_right(b)))
+            def _():
+                r_copy(b, a, 0, right).start()
 
         for b in (0, 1):
             if t > 0:
-                got = (z <= last) if b == 0 else jnp.logical_and(z <= last, p >= group)
+                got = is_z if b == 0 else jnp.logical_and(is_z, p >= group)
 
                 @pl.when(got)
                 def _():
-                    r_copy(b, z0, 1, right).wait_recv()
-
-                @pl.when(jnp.logical_and(got, jnp.logical_and(odd == 0, r == b)))
-                def _():
-                    f_copy(0, z0).start()
-
-            @pl.when(jnp.logical_and(z <= last, moves_left(b)))
-            def _():
-                r_copy(b, z0, 1, left).start()
-
+                    r_copy(b, z, 1, right).wait_recv()
+
+                forward(0, z, jnp.logical_and(got, r == b))
+
+            @pl.when(jnp.logical_and(is_z, moves_left(b)))
+            def _():
+                r_copy(b, z, 1, left).start()
+
+    def relay_c(t):
+        is_a, a, is_z, z = places(t)
         if t > 0:
-            @pl.when(a >= 0)
-            def _():
-                c_copy(a0, 0, left).wait_recv()
-
-            @pl.when(jnp.logical_and(a >= 0, odd == 0))
-            def _():
-                f_copy(1, a0).start()
-
-        @pl.when(jnp.logical_and(a >= 0, p < last))
-        def _():
-            c_copy(a0, 0, right).start()
+            @pl.when(is_a)
+            def _():
+                c_copy(a, 0, left).wait_recv()
+
+            forward(1, a, is_a)
+
+        @pl.when(jnp.logical_and(is_a, p < last))
+        def _():
+            c_copy(a, 0, right).start()
 
         if t > 0:
-            @pl.when(z <= last)
-            def _():
-                c_copy(z0, 1, right).wait_recv()
-
-            @pl.when(jnp.logical_and(z <= last, odd == 0))
-            def _():
-                f_copy(1, z0).start()
-
-        @pl.when(jnp.logical_and(z <= last, p > 0))
-        def _():
-            c_copy(z0, 1, left).start()
-
-        if t == 0:
+            @pl.when(is_z)
+            def _():
+                c_copy(z, 1, right).wait_recv()
+
+            forward(1, z, is_z)
+
+        @pl.when(jnp.logical_and(is_z, p > 0))
+        def _():
+            c_copy(z, 1, left).start()
+
+    tall_chunk = min(256, height)
+
+    def tall_lines(i):
+        return pl.ds(pl.multiple_of(i * tall_chunk, tall_chunk), tall_chunk)
+
+    def line_products():
+        @pl.when(odd == 1)
+        def _():
+            for q in range(n_c):
+                f_copy(0, q).wait_recv()
+
+        def some(i, _):
+            @pl.when(odd == 1)
+            def _():
+                re, im = times(
+                    rhs_full[r, :, tall_lines(i), :].reshape(2 * tall_chunk, cols),
+                    line_ref[0, 0, :, part(h)], line_ref[0, 1, :, part(h)],
+                )
+                direct[0, tall_lines(i), :] = re
+                direct[1, tall_lines(i), :] = im
+                src[:, tall_lines(i), :] = r_in[:, tall_lines(i), :]
+
             @pl.when(odd == 0)
             def _():
-                f_copy(0, p).start()
-                f_copy(1, p).start()
-
-            weights()
+                src[:, tall_lines(i), :] = rhs_full[r, :, tall_lines(i), :]
+
+            re, im = times(src[:, tall_lines(i), :].reshape(2 * tall_chunk, cols), weight[0], weight[1])
+            mixed[odd, 0, tall_lines(i), :] = re.astype(BF)
+            mixed[odd, 1, tall_lines(i), :] = im.astype(BF)
+            return 0
+
+        lax.fori_loop(0, height // tall_chunk, some, 0)
+
+    relay_r(0)
+    relay_c(0)
+    forward(0, p, p >= 0)
+    forward(1, p, p >= 0)
+    weights()
+    for t in range(1, n_c):
+        relay_r(t)
+    relay_c(1)
+    line_products()
+    for t in range(2, n_c):
+        relay_c(t)
 
     def padded_lines(i):
         return pl.ds(pl.multiple_of(PAD + i * chunk, PAD), chunk)
@@ -246,25 +283,56 @@
 
     @pl.when(odd == 1)
     def _():
-        def own_lines(i, _):
-            re, im = times(
-                rhs_full[r, :, lines(i), :].reshape(2 * chunk, cols), line_ref[0, 0, :, part(h)], line_ref[0, 1, :, part(h)]
-            )
+        for q in range(n_c):
+            f_copy(1, q).wait_recv()
+
+        def even_layer(i, _):
+            re, im = times(c_in[:, tall_lines(i), :].reshape(2 * tall_chunk, height), mixed[1, 0], mixed[1, 1])
+            mixed[0, 0, tall_lines(i), :] = (direct[0, tall_lines(i), :] + re).astype(BF)
+            mixed[0, 1, tall_lines(i), :] = (direct[1, tall_lines(i), :] + im).astype(BF)
+            return 0
+
+        lax.fori_loop(0, height // tall_chunk, even_layer, 0)
+
+    hands_on = jnp.logical_and(odd == 1, sec <= n_s - 3)
+
+    def put(i, re, im):
+        o_buf[h, 0, padded_lines(i), :] = re.astype(BF)
+        o_buf[h, 1, padded_lines(i), :] = im.astype(BF)
+
+        @pl.when(hands_on)
+        def _():
+            s_copy(i).start()
+
+    def alone(i, _):
+        re, im = times(c_full[:, lines(i), :].reshape(2 * chunk, height), mixed[0, 0], mixed[0, 1])
+
+        @pl.when(sec < 2)
+        def _():
+            put(i, re, im)
+
+        @pl.when(sec >= 2)
+        def _():
             direct[0, lines(i), :] = re
             direct[1, lines(i), :] = im
-            return 0
-
-        lax.fori_loop(0, chunks, own_lines, 0)
-        for q in range(n_c):
-            f_copy(0, q).wait_recv()
-
-    @pl.when(odd == 0)
-    def _():
-        r_in[...] = rhs_full[r]
-
-    def take(i, _):
-        @pl.when(sec >= 2)
-        def _():
+
+            @pl.when(odd == 0)
+            def _():
+                both[:, lines(i), :] = c_full[:, lines(i), :]
+
+            @pl.when(odd == 1)
+            def _():
+                re, im = times(c_full[:, lines(i), :].reshape(2 * chunk, height), c_in[0], c_in[1])
+                both[0, lines(i), :] = re.astype(BF)
+                both[1, lines(i), :] = im.astype(BF)
+
+        return 0
+
+    lax.fori_loop(0, chunks, alone, 0)
+
+    @pl.when(sec >= 2)
+    def _():
+        def take(i, _):
             d_copy(i, h).wait_recv()
 
             @pl.when(odd == 1)
@@ -283,49 +351,20 @@
 
             for c in range(2):
                 for j in range(group):
-                    at = slice(j * width, (j + 1) * width)
-                    src[c, :, at] = (
-                        r_in[c, lines(i), at].astype(jnp.float32) + s_in[j, c, lines(i), :].astype(jnp.float32)
-                    ).astype(BF)
-
-        @pl.when(sec < 2)
-        def _():
-            src[...] = r_in[:, lines(i), :]
-
-        re, im = times(src[...].reshape(2 * chunk, cols), weight[0], weight[1])
-        mixed[odd, 0, lines(i), :] = re.astype(BF)
-        mixed[odd, 1, lines(i), :] = im.astype(BF)
-        return 0
-
-    lax.fori_loop(0, chunks, take, 0)
-
-    @pl.when(odd == 1)
-    def _():
-        for q in range(n_c):
-            f_copy(1, q).wait_recv()
-
-        def even_layer(i, _):
-            re, im = times(c_in[:, lines(i), :].reshape(2 * chunk, height), mixed[1, 0], mixed[1, 1])
-            mixed[0, 0, lines(i), :] = (direct[0, lines(i), :] + re).astype(BF)
-            mixed[0, 1, lines(i), :] = (direct[1, lines(i), :] + im).astype(BF)
+                    src[c, lines(i), j * width : (j + 1) * width] = s_in[j, c, lines(i), :]
+            re, im = times(src[:, lines(i), :].reshape(2 * chunk, cols), weight[0], weight[1])
+            mixed[0, 0, lines(i), :] = re.astype(BF)
+            mixed[0, 1, lines(i), :] = im.astype(BF)
             return 0
 
-        lax.fori_loop(0, chunks, even_layer, 0)
-
-    hands_on = jnp.logical_and(odd == 1, sec <= n_s - 3)
-
-    def give(i, _):
-        re, im = times(c_full[:, lines(i), :].reshape(2 * chunk, height), mixed[0, 0], mixed[0, 1])
-        o_buf[h, 0, padded_lines(i), :] = re.astype(BF)
-        o_buf[h, 1, padded_lines(i), :] = im.astype(BF)
-
-        @pl.when(hands_on)
-        def _():
-            s_copy(i).start()
-
-        return 0
-
-    lax.fori_loop(0, chunks, give, 0)
+        lax.fori_loop(0, chunks, take, 0)
+
+        def give(i, _):
+            re, im = times(both[:, lines(i), :].reshape(2 * chunk, height), mixed[0, 0], mixed[0, 1])
+            put(i, direct[0, lines(i), :] + re, direct[1, lines(i), :] + im)
+            return 0
+
+        lax.fori_loop(0, chunks, give, 0)
 
     tall = rows + 2 * PAD
 
@@ -400,28 +439,23 @@
         neighbour(1)
 
     for t in range(n_c):
-        a = p - t
-        a0 = jnp.maximum(a, 0)
-        z = p + t
-        z0 = jnp.minimum(z, last)
-        right = jnp.minimum(p + 1, last)
-        left = jnp.maximum(p - 1, 0)
+        is_a, a, is_z, z = places(t)
         for b in range(RHS):
-            @pl.when(jnp.logical_and(a >= 0, moves_right(b)))
-            def _():
-                r_copy(b, a0, 0, right).wait_send()
-
-            @pl.when(jnp.logical_and(z <= last, moves_left(b)))
-            def _():
-                r_copy(b, z0, 1, left).wait_send()
-
-        @pl.when(jnp.logical_and(a >= 0, p < last))
-        def _():
-            c_copy(a0, 0, right).wait_send()
-
-        @pl.when(jnp.logical_and(z <= last, p > 0))
-        def _():
-            c_copy(z0, 1, left).wait_send()
+            @pl.when(jnp.logical_and(is_a, moves_right(b)))
+            def _():
+                r_copy(b, a, 0, right).wait_send()
+
+            @pl.when(jnp.logical_and(is_z, moves_left(b)))
+            def _():
+                r_copy(b, z, 1, left).wait_send()
+
+        @pl.when(jnp.logical_and(is_a, p < last))
+        def _():
+            c_copy(a, 0, right).wait_send()
+
+        @pl.when(jnp.logical_and(is_z, p > 0))
+        def _():
+            c_copy(z, 1, left).wait_send()
 
     def sent(i, _):
         @pl.when(hands_on)
@@ -480,7 +514,8 @@
             pltpu.VMEM((2, cols, cols), BF),
             pltpu.VMEM((2, cols, width), BF),
             pltpu.VMEM((2, height, width), jnp.float32),
-            pltpu.VMEM((2, chunk, cols), BF),
+            pltpu.VMEM((2, height, cols), BF),
+            pltpu.VMEM((2, height, height), BF),
             pltpu.VMEM((2, 2, height, width), BF),
             pltpu.VMEM((group, 2, height, width), BF),
             pltpu.VMEM((group, 2, height + 2 * PAD, width), BF),

time: 142 us -> 131 us (0.923)
  Pallas kernels: 137 us -> 126 us
    pallas_call x1, Pallas kernels: 137 us -> 126 us  [per_device(): pl.pallas_call(functools.partial(kernel, n_s, n_c), out_shape=(out, out),...]
where the time goes in v3:
time: 131 us
  Pallas kernels  126 us (96%)
  local copies, waits for them, and re-layouts  3.32 us (3%)
    pallas_call x1, Pallas kernels, per_device(): pl.pallas_call(functools.partial(kernel, n_s, n_c), out_shape=(out, out),...  126 us
    unnamed x4, local copies, waits for them, and re-layouts  3.32 us

profile of v3, /device:TPU:29, one launch (start us, length us, event | category | flops | bytes accessed | tf_op | source)
XLA Modules:
  0.0 130.5 jit_solution(6114194737757939838)
XLA Ops:
  1.3 125.9 %sweep.1 = (f32[2,1,2,128,512]{4,3,2,1,0:T(8,128)}, f32[2,1,2,128,512]{4,3,2,1,0:T(8,128)}) custom-call(f32[2,1,2,128,512]{4,3,2,1,0:T(8,128)} %rhs_ref.1, f32[1,128,512]{2,1,0:T(8,128)} %slow_ref.1, s32[1]{0:T(128)S(6)} %copy.9.depth_ref, bf16[1,2,512,512]{3,2,1,0:T(8,128)(2,1)} %line_ref.1, bf16[1,2,128,512]{3,2,1,0:T(8,128)(2,1)} %cross_ref.1), custom_call_target="tpu_custom_call" | custom-call | tf_op jit(solution)/shard_map/sweep/pallas_call | solution.py:504
  127.2 0.0 copy-start
  127.2 2.4 %copy.10 = f32[2,1,2,128,512]{4,3,2,1,0:T(8,128)} copy(f32[2,1,2,128,512]{4,3,2,1,0:T(8,128)} %get-tuple-element.4) | data formatting | bytes 2097152
  129.6 0.0 copy-done
  129.6 1.0 copy.11
Async XLA Ops:
  127.2 2.4 %copy-start = (f32[2,1,2,128,512]{4,3,2,1,0:T(8,128)S(1)}, f32[2,1,2,128,512]{4,3,2,1,0:T(8,128)}, u32[]{:S(2)}) copy-start(f32[2,1,2,128,512]{4,3,2,1,0:T(8,128)} %get-tuple-element.5) | copy-start | bytes 3145732

commit v4 on v3

--- a/solution.py
+++ b/solution.py
@@ -294,6 +294,14 @@
 
         lax.fori_loop(0, height // tall_chunk, even_layer, 0)
 
+    tall = rows + 2 * PAD
+
+    def own(q):
+        return pl.ds(pl.multiple_of(q * rows, PAD), tall)
+
+    def e_copy(to, whose):
+        return remote(o_buf.at[h, :, own(to), :], ext.at[whose], e_send.at[to], e_recv.at[whose], at_cross(to))
+
     hands_on = jnp.logical_and(odd == 1, sec <= n_s - 3)
 
     def put(i, re, im):
@@ -304,6 +312,13 @@
         def _():
             s_copy(i).start()
 
+        for q in range(n_c):
+            complete = min(((q + 1) * rows + PAD - 1) // chunk, chunks - 1)
+
+            @pl.when(jnp.logical_and(i == complete, p != q))
+            def _():
+                e_copy(q, p).start()
+
     def alone(i, _):
         re, im = times(c_full[:, lines(i), :].reshape(2 * chunk, height), mixed[0, 0], mixed[0, 1])
 
@@ -332,7 +347,7 @@
 
     @pl.when(sec >= 2)
     def _():
-        def take(i, _):
+        def pass_on(i, _):
             d_copy(i, h).wait_recv()
 
             @pl.when(odd == 1)
@@ -341,6 +356,11 @@
                     y_copy(i, d).start()
                 d_copy(i, h).start()
 
+            return 0
+
+        lax.fori_loop(0, chunks, pass_on, 0)
+
+        def take(i, _):
             for d in range(1, group):
                 j = (h + d) % group
                 d_copy(i, j).wait_recv()
@@ -366,21 +386,12 @@
 
         lax.fori_loop(0, chunks, give, 0)
 
-    tall = rows + 2 * PAD
-
-    def own(q):
-        return pl.ds(pl.multiple_of(q * rows, PAD), tall)
-
-    def e_copy(d):
-        q = (p + d) % n_c
-        return remote(o_buf.at[h, :, own(q), :], ext.at[p], e_send.at[d], e_recv.at[p], at_cross(q))
-
-    for d in range(1, n_c):
-        e_copy(d).start()
+    for q in range(n_c):
+        @pl.when(p != q)
+        def _():
+            e_copy(q, q).wait_recv()
+
     ext[p] = o_buf[h, :, own(p), :]
-    for d in range(1, n_c):
-        q = (p + d) % n_c
-        remote(o_buf.at[h, :, own(q), :], ext.at[q], e_send.at[d], e_recv.at[q], at_cross(q)).wait_recv()
 
     column = lax.broadcasted_iota(jnp.int32, (rows, cols), 1)
 
@@ -479,8 +490,11 @@
             f_copy(1, q).wait_send()
 
     lax.fori_loop(0, chunks, sent, 0)
-    for d in range(1, n_c):
-        e_copy(d).wait_send()
+    for q in range(n_c):
+        @pl.when(p != q)
+        def _():
+            e_copy(q, p).wait_send()
+
 
     @pl.when(sec < n_s - 1)
     def _():

time: 131 us -> 114 us (0.87)
  Pallas kernels: 126 us -> 109 us
    pallas_call x1, Pallas kernels: 126 us -> 109 us  [per_device(): pl.pallas_call(functools.partial(kernel, n_s, n_c), out_shape=(out, out),...]
where the time goes in v4:
time: 114 us
  Pallas kernels  109 us (96%)
  local copies, waits for them, and re-layouts  3.32 us (3%)
  between operations  1.29 us (1%)
    pallas_call x1, Pallas kernels, per_device(): pl.pallas_call(functools.partial(kernel, n_s, n_c), out_shape=(out, out),...  109 us
    unnamed x4, local copies, waits for them, and re-layouts  3.32 us

profile of v4, /device:TPU:29, one launch (start us, length us, event | category | flops | bytes accessed | tf_op | source)
XLA Modules:
  0.0 114.0 jit_solution(15688230233532763280)
XLA Ops:
  1.3 109.3 %sweep.1 = (f32[2,1,2,128,512]{4,3,2,1,0:T(8,128)}, f32[2,1,2,128,512]{4,3,2,1,0:T(8,128)}) custom-call(f32[2,1,2,128,512]{4,3,2,1,0:T(8,128)} %rhs_ref.1, f32[1,128,512]{2,1,0:T(8,128)} %slow_ref.1, s32[1]{0:T(128)S(6)} %copy.9.depth_ref, bf16[1,2,512,512]{3,2,1,0:T(8,128)(2,1)} %line_ref.1, bf16[1,2,128,512]{3,2,1,0:T(8,128)(2,1)} %cross_ref.1), custom_call_target="tpu_custom_call" | custom-call | tf_op jit(solution)/shard_map/sweep/pallas_call | solution.py:518
  110.6 0.0 copy-start
  110.6 2.4 %copy.10 = f32[2,1,2,128,512]{4,3,2,1,0:T(8,128)} copy(f32[2,1,2,128,512]{4,3,2,1,0:T(8,128)} %get-tuple-element.4) | data formatting | bytes 2097152
  113.0 0.0 copy-done
  113.0 1.0 copy.11
Async XLA Ops:
  110.6 2.4 %copy-start = (f32[2,1,2,128,512]{4,3,2,1,0:T(8,128)S(1)}, f32[2,1,2,128,512]{4,3,2,1,0:T(8,128)}, u32[]{:S(2)}) copy-start(f32[2,1,2,128,512]{4,3,2,1,0:T(8,128)} %get-tuple-element.5) | copy-start | bytes 3145732

commit v5 on v4

--- a/solution.py
+++ b/solution.py
@@ -331,6 +331,24 @@
             direct[0, lines(i), :] = re
             direct[1, lines(i), :] = im
 
+        return 0
+
+    lax.fori_loop(0, chunks, alone, 0)
+
+    @pl.when(sec >= 2)
+    def _():
+        def pass_on(i, _):
+            d_copy(i, h).wait_recv()
+
+            @pl.when(odd == 1)
+            def _():
+                for d in range(1, group):
+                    y_copy(i, d).start()
+                d_copy(i, h).start()
+
+            return 0
+
+        def compose(i, _):
             @pl.when(odd == 0)
             def _():
                 both[:, lines(i), :] = c_full[:, lines(i), :]
@@ -341,24 +359,17 @@
                 both[0, lines(i), :] = re.astype(BF)
                 both[1, lines(i), :] = im.astype(BF)
 
-        return 0
-
-    lax.fori_loop(0, chunks, alone, 0)
-
-    @pl.when(sec >= 2)
-    def _():
-        def pass_on(i, _):
-            d_copy(i, h).wait_recv()
-
-            @pl.when(odd == 1)
-            def _():
-                for d in range(1, group):
-                    y_copy(i, d).start()
-                d_copy(i, h).start()
-
             return 0
 
-        lax.fori_loop(0, chunks, pass_on, 0)
+        @pl.when(sec < 4)
+        def _():
+            lax.fori_loop(0, chunks, pass_on, 0)
+
+        lax.fori_loop(0, chunks, compose, 0)
+
+        @pl.when(sec >= 4)
+        def _():
+            lax.fori_loop(0, chunks, pass_on, 0)
 
         def take(i, _):
             for d in range(1, group):

time: 114 us -> 114 us (level)
  no operation moved by 1% of the time
where the time goes in v5:
time: 114 us
  Pallas kernels  109 us (96%)
  local copies, waits for them, and re-layouts  3.32 us (3%)
  between operations  1.29 us (1%)
    pallas_call x1, Pallas kernels, per_device(): pl.pallas_call(functools.partial(kernel, n_s, n_c), out_shape=(out, out),...  109 us
    unnamed x4, local copies, waits for them, and re-layouts  3.32 us

profile of v5, /device:TPU:29, one launch (start us, length us, event | category | flops | bytes accessed | tf_op | source)
XLA Modules:
  0.0 114.1 jit_solution(3400752311551237029)
XLA Ops:
  1.3 109.5 %sweep.1 = (f32[2,1,2,128,512]{4,3,2,1,0:T(8,128)}, f32[2,1,2,128,512]{4,3,2,1,0:T(8,128)}) custom-call(f32[2,1,2,128,512]{4,3,2,1,0:T(8,128)} %rhs_ref.1, f32[1,128,512]{2,1,0:T(8,128)} %slow_ref.1, s32[1]{0:T(128)S(6)} %copy.9.depth_ref, bf16[1,2,512,512]{3,2,1,0:T(8,128)(2,1)} %line_ref.1, bf16[1,2,128,512]{3,2,1,0:T(8,128)(2,1)} %cross_ref.1), custom_call_target="tpu_custom_call" | custom-call | tf_op jit(solution)/shard_map/sweep/pallas_call | solution.py:529
  110.8 0.0 copy-start
  110.8 2.4 %copy.10 = f32[2,1,2,128,512]{4,3,2,1,0:T(8,128)} copy(f32[2,1,2,128,512]{4,3,2,1,0:T(8,128)} %get-tuple-element.4) | data formatting | bytes 2097152
  113.1 0.0 copy-done
  113.1 1.0 copy.11
Async XLA Ops:
  110.8 2.4 %copy-start = (f32[2,1,2,128,512]{4,3,2,1,0:T(8,128)S(1)}, f32[2,1,2,128,512]{4,3,2,1,0:T(8,128)}, u32[]{:S(2)}) copy-start(f32[2,1,2,128,512]{4,3,2,1,0:T(8,128)} %get-tuple-element.5) | copy-start | bytes 3145732
